TPU v7x, 768 devices: a whole 4x8x12 slice. The times are simulated.
768 devices in a mesh: fsdp: 96 (over x, y_lo, z), island: 8 (over y_hi, core).
Axes of the slice: x: 4, y: 8 (y_hi: 4, y_lo: 2; y = y_hi * 2 + y_lo), z: 12, core: 2. Of those that a mesh axis runs over, the one named last changes fastest.
Arguments:
- acts: bfloat16 [8, 24576, 4096], P('island', 'fsdp'), may hold values from -6 to 6
- grad_out: bfloat16 [8, 24576, 128], P('island', 'fsdp'), may hold values from -0.15234375 to 0.15234375
- params: float32 [8, 4128, 128], P('island', 'fsdp'), may hold values from -3 to 3
- adam_m: float32 [8, 4128, 128], P('island', 'fsdp'), may hold values from -4 to 4
- adam_v: float32 [8, 4128, 128], P('island', 'fsdp'), may hold values from 0.01 to 16
- global_params: float32 [4128, 128], P('fsdp'), may hold values from -3 to 3
- outer_mom: float32 [4128, 128], P('fsdp'), may hold values from -2 to 2
Outputs:
- mixed: float32 [8, 4128, 128], P('island', 'fsdp')
- first_moment: float32 [8, 4128, 128], P('island', 'fsdp')
- second_moment: float32 [8, 4128, 128], P('island', 'fsdp')
- new_global: float32 [4128, 128], P('fsdp')
- new_mom: float32 [4128, 128], P('fsdp')
- forward_weight: bfloat16 [8, 4096, 128], P('island')
All inputs are finite; a program needn't handle non-finite values.
Results may differ from a plain program's by a relative error of at most 0.0004.
Values may be sent and summed in bfloat16 or wider, within the bound.
No kernel may reach another device: no remote copies, remote signals or barrier semaphores. Data moves between devices by JAX's collectives and lax.ppermute only.
A program may use at most 32 MiB of HBM per device.

v0:
```python
import jax
import jax.numpy as jnp
from jax import lax
from jax.sharding import PartitionSpec as P

INNER_STEP = 100


beta_one = 0.9
beta_two = 0.95
epsilon = 1e-08
inner_rate = 0.001
decay_rate = 0.1
outer_rate = 0.7
momentum = 0.9
mixing = 0.5


def on_device(acts, grad_out, params, adam_m, adam_v, global_params, outer_mom):
    shard_rows = params.shape[1]
    features = acts.shape[2]
    padded_rows = shard_rows * lax.axis_size("fsdp")
    islands = lax.axis_size("island")
    inputs = acts[0]
    cotangent = grad_out[0]
    whole = jnp.einsum("td,th->dh", inputs, cotangent, preferred_element_type=jnp.float32)
    whole = jnp.pad(whole, ((0, padded_rows - features), (0, 0)))
    gradient = lax.psum_scatter(whole, "fsdp", scatter_dimension=0, tiled=True)
    gradient = gradient[None]
    first_moment = beta_one * adam_m + (1.0 - beta_one) * gradient
    second_moment = beta_two * adam_v + (1.0 - beta_two) * gradient * gradient
    first_hat = first_moment / (1.0 - beta_one**INNER_STEP)
    second_hat = second_moment / (1.0 - beta_two**INNER_STEP)
    inner = params - inner_rate * (
        first_hat / (jnp.sqrt(second_hat) + epsilon) + decay_rate * params
    )
    summed = lax.psum(global_params[None] - inner, "island")
    delta = summed[0] / islands
    new_mom = momentum * outer_mom + delta
    new_global = global_params - outer_rate * (delta + momentum * new_mom)
    mixed = mixing * inner + (1.0 - mixing) * new_global[None]
    gathered = lax.all_gather(mixed.astype(jnp.bfloat16), "fsdp", axis=1, tiled=True)
    forward_weight = gathered[:, :features]
    return (mixed, first_moment, second_moment, new_global, new_mom, forward_weight)


def solution(mesh):
    in_specs = (
        P("island", "fsdp", None),
        P("island", "fsdp", None),
        P("island", "fsdp", None),
        P("island", "fsdp", None),
        P("island", "fsdp", None),
        P("fsdp", None),
        P("fsdp", None),
    )
    out_specs = (
        P("island", "fsdp", None),
        P("island", "fsdp", None),
        P("island", "fsdp", None),
        P("fsdp", None),
        P("fsdp", None),
        P("island", None, None),
    )
    return jax.shard_map(
        on_device, mesh=mesh, in_specs=in_specs, out_specs=out_specs, check_vma=False
    )
```

profile of v0, /device:TPU:16, one launch (start us, length us, event | category | flops | bytes accessed | tf_op | source)
XLA Modules:
  0.0 805.1 jit_solution(8943125568190305982)
XLA Ops:
  7.2 0.0 copy-start
  7.2 0.0 all-gather.2.cloned.1.call-start
  7.2 1.5 copy-done
  8.8 1.6 fusion.1
  10.4 1.5 pad.4
  11.9 0.0 copy-start.3
  11.9 255.9 %fusion = f32[48,128]{1,0:T(8,128)S(1)} fusion(f32[4128,128]{1,0:T(8,128)} %pad.4), kind=kCustom, calls=%all-reduce-scatter | all-reduce-scatter fusion | flops 589825 | bytes 2142208
  267.8 1.3 collective-permute-start.8
  269.1 1.3 collective-permute-start.7
  270.4 1.3 collective-permute-start.6
  271.7 1.3 collective-permute-start.5
  273.0 1.3 collective-permute-start.9
  274.3 1.5 collective-permute-done.9
  275.8 1.3 collective-permute-start.4
  277.1 0.0 collective-permute-done.8
  277.1 1.3 collective-permute-start.3
  278.4 0.0 collective-permute-done.7
  278.4 10.6 %collective-permute-start.2 = (f32[48,128]{1,0:T(8,128)S(1)}, f32[48,128]{1,0:T(8,128)S(1)}, u32[]{:S(2)}, u32[]{:S(2)}) collective-permute-start(f32[48,128]{1,0:T(8,128)S(1)} %fusion), channel_id=1, source_target_pairs={{0,24},{8,32},{16,40},{24,48},{32,56},{40,64},{48,72},{56,80},{64,... | collective-permute-start | bytes 73736
  289.0 4.3 collective-permute-start.1
  293.3 2.5 collective-permute-start
  295.7 1.3 dynamic-slice.4
  297.7 1.5 concatenate
  299.3 24.6 %psum.7 = f32[1,43,128]{2,1,0:T(8,128)S(1)} all-reduce(f32[1,43,128]{2,1,0:T(8,128)S(1)} %get-tuple-element.22), channel_id=1, replica_groups=mesh['fsdp'=96,'island'=8] {'island'}, use_global_device_ids=true, to_apply=%region_1.2 | all-reduce | flops 5504 | bytes 44032 | tf_op jit(solution)/shard_map/psum | solution.py:37
  323.9 0.6 fusion.9
  324.5 0.6 copy.24
  325.2 0.0 all-gather.2.cloned.1.call-update
  325.2 0.6 copy.26
  325.8 0.6 copy.27
  326.4 0.6 copy.25
  327.1 468.5 %all-gather.2.cloned.1.call-done = bf16[1,4128,128]{2,0,1:T(2,128)(2,1)} async-done(((bf16[1,43,128]{2,0,1:T(2,128)(2,1)}), bf16[1,4128,128]{2,0,1:T(2,128)(2,1)}) %all-gather.2.cloned.1.call-update) | async-done | bytes 1056784 | tf_op jit(solution)/shard_map/all_gather | solution.py:42
  795.5 1.6 slice-done
  797.1 1.1 copy.28
  (19 shorter events, 0.1 us)
Async XLA Ops:
  7.2 1.6 copy-start
  7.2 788.4 %all-gather.2.cloned.1.call-start = ((), (), s32[]{:S(2)}) async-start(), calls=%async_computation | async-start | bytes 2135552 | tf_op jit(solution)/shard_map/all_gather | solution.py:42
  11.8 287.4 %copy-start.1 = (f32[43,128]{1,0:T(8,128)S(1)}, f32[43,128]{1,0:T(8,128)}, u32[]{:S(2)}) copy-start(f32[43,128]{1,0:T(8,128)} %param.12) | copy-start | bytes 66052
  11.8 287.4 %copy-start.2 = (f32[1,43,128]{2,0,1:T(1,128)S(1)}, f32[1,43,128]{2,0,1:T(1,128)}, u32[]{:S(2)}) copy-start(f32[1,43,128]{2,0,1:T(1,128)} %param.9) | copy-start | bytes 66052
  11.9 287.4 %copy-start.4 = (f32[1,43,128]{2,0,1:T(1,128)S(1)}, f32[1,43,128]{2,0,1:T(1,128)}, u32[]{:S(2)}) copy-start(f32[1,43,128]{2,0,1:T(1,128)} %param.10) | copy-start | bytes 66052
  11.9 287.4 %copy-start.5 = (f32[1,43,128]{2,0,1:T(1,128)S(1)}, f32[1,43,128]{2,0,1:T(1,128)}, u32[]{:S(2)}) copy-start(f32[1,43,128]{2,0,1:T(1,128)} %param.11) | copy-start | bytes 66052
  11.9 312.0 %copy-start.3 = (f32[43,128]{1,0:T(8,128)S(1)}, f32[43,128]{1,0:T(8,128)}, u32[]{:S(2)}) copy-start(f32[43,128]{1,0:T(8,128)} %param.13) | copy-start | bytes 66052
  267.8 9.3 %collective-permute-start.8 = (f32[48,128]{1,0:T(8,128)S(1)}, f32[48,128]{1,0:T(8,128)S(1)}, u32[]{:S(2)}, u32[]{:S(2)}) collective-permute-start(f32[48,128]{1,0:T(8,128)S(1)} %fusion), channel_id=1, source_target_pairs={{0,72},{8,80},{16,88},{24,96},{32,104},{40,112},{48,120},{56,128},... | collective-permute-start | bytes 73736
  269.1 9.3 %collective-permute-start.7 = (f32[48,128]{1,0:T(8,128)S(1)}, f32[48,128]{1,0:T(8,128)S(1)}, u32[]{:S(2)}, u32[]{:S(2)}) collective-permute-start(f32[48,128]{1,0:T(8,128)S(1)} %fusion), channel_id=1, source_target_pairs={{0,64},{8,72},{16,80},{24,88},{32,96},{40,104},{48,112},{56,120},{... | collective-permute-start | bytes 73736
  270.4 18.6 %collective-permute-start.6 = (f32[48,128]{1,0:T(8,128)S(1)}, f32[48,128]{1,0:T(8,128)S(1)}, u32[]{:S(2)}, u32[]{:S(2)}) collective-permute-start(f32[48,128]{1,0:T(8,128)S(1)} %fusion), channel_id=1, source_target_pairs={{0,56},{8,64},{16,72},{24,80},{32,88},{40,96},{48,104},{56,112},{6... | collective-permute-start | bytes 73736
  271.7 21.6 %collective-permute-start.5 = (f32[48,128]{1,0:T(8,128)S(1)}, f32[48,128]{1,0:T(8,128)S(1)}, u32[]{:S(2)}, u32[]{:S(2)}) collective-permute-start(f32[48,128]{1,0:T(8,128)S(1)} %fusion), channel_id=1, source_target_pairs={{0,48},{8,56},{16,64},{24,72},{32,80},{40,88},{48,96},{56,104},{64... | collective-permute-start | bytes 73736
  273.0 2.8 collective-permute-start.9
  275.8 21.9 %collective-permute-start.4 = (f32[48,128]{1,0:T(8,128)S(1)}, f32[48,128]{1,0:T(8,128)S(1)}, u32[]{:S(2)}, u32[]{:S(2)}) collective-permute-start(f32[48,128]{1,0:T(8,128)S(1)} %fusion), channel_id=1, source_target_pairs={{0,40},{8,48},{16,56},{24,64},{32,72},{40,80},{48,88},{56,96},{64,... | collective-permute-start | bytes 73736
  277.1 20.6 %collective-permute-start.3 = (f32[48,128]{1,0:T(8,128)S(1)}, f32[48,128]{1,0:T(8,128)S(1)}, u32[]{:S(2)}, u32[]{:S(2)}) collective-permute-start(f32[48,128]{1,0:T(8,128)S(1)} %fusion), channel_id=1, source_target_pairs={{0,32},{8,40},{16,48},{24,56},{32,64},{40,72},{48,80},{56,88},{64,... | collective-permute-start | bytes 73736
  278.4 19.3 %collective-permute-start.2 = (f32[48,128]{1,0:T(8,128)S(1)}, f32[48,128]{1,0:T(8,128)S(1)}, u32[]{:S(2)}, u32[]{:S(2)}) collective-permute-start(f32[48,128]{1,0:T(8,128)S(1)} %fusion), channel_id=1, source_target_pairs={{0,24},{8,32},{16,40},{24,48},{32,56},{40,64},{48,72},{56,80},{64,... | collective-permute-start | bytes 73736
  289.0 8.7 %collective-permute-start.1 = (f32[48,128]{1,0:T(8,128)S(1)}, f32[48,128]{1,0:T(8,128)S(1)}, u32[]{:S(2)}, u32[]{:S(2)}) collective-permute-start(f32[48,128]{1,0:T(8,128)S(1)} %fusion), channel_id=1, source_target_pairs={{0,16},{8,24},{16,32},{24,40},{32,48},{40,56},{48,64},{56,72},{64,... | collective-permute-start | bytes 73736
  293.3 4.5 collective-permute-start
  795.5 1.6 slice-start
Sparse Core Ops, SparseCore 0:
  325.3 470.1 all-gather.1
where the time goes:
time: 806 us; the launch traced here: 805 us
  waiting for transfers between devices  470 us (58%)
  blocking collectives  280 us (35%)
  starting transfers between devices  26.3 us (3%)
  between operations  14.9 us (2%)
  local copies, waits for them, and re-layouts  11.1 us (1%)
    all_gather x1, waiting for transfers between devices, on_device(): lax.all_gather(mixed.astype(jnp.bfloat16), 'fsdp', axis=1, tiled=True)  468 us
    unnamed x1, blocking collectives  256 us
    unnamed x10, starting transfers between devices  26.3 us
    psum x1, blocking collectives, on_device(): summed = lax.psum(global_params[None] - inner, 'island')  24.6 us
  transfers between devices with their start and end apart: 11, of which 2 were waited for; matrix products, arithmetic and copies ran while one was open for 0% of the time, Pallas kernels for 0%

commit v1 on v0

v1 whole, which is shorter than its diff:
```python
import jax
import jax.numpy as jnp
from jax import lax
from jax.sharding import Mesh
from jax.sharding import PartitionSpec as P

INNER_STEP = 100


beta_one = 0.9
beta_two = 0.95
epsilon = 1e-08
inner_rate = 0.001
decay_rate = 0.1
outer_rate = 0.7
momentum = 0.9
mixing = 0.5

X, Y_LO, Z, Y_HI, CORE = 4, 2, 12, 4, 2
PLANE = ("x", "y_lo")
FSDP = ("x", "y_lo", "z")
ISLAND = ("y_hi", "core")


def to_every(block, axes, count):
    copies = jnp.broadcast_to(block[None], (count, *block.shape))
    return lax.all_to_all(copies, axes, 0, 0)


def on_device(acts, grad_out, params, adam_m, adam_v, global_params, outer_mom):
    shard_rows = params.shape[1]
    features = acts.shape[2]
    width = params.shape[2]
    plane, islands = X * Y_LO, Y_HI * CORE
    padded_rows = shard_rows * plane * Z
    whole = jnp.einsum("td,th->dh", acts[0], grad_out[0], preferred_element_type=jnp.float32)
    whole = jnp.pad(whole, ((0, padded_rows - features), (0, 0)))
    sent = whole.reshape(plane, Z * shard_rows, width).astype(jnp.float16)
    got = lax.all_to_all(sent, PLANE, 0, 0)
    part = jnp.sum(got.astype(jnp.float32), axis=0)
    sent = part.reshape(Z, shard_rows, width).astype(jnp.float16)
    got = lax.all_to_all(sent, "z", 0, 0)
    gradient = jnp.sum(got.astype(jnp.float32), axis=0)
    first_moment = beta_one * adam_m[0] + (1.0 - beta_one) * gradient
    second_moment = beta_two * adam_v[0] + (1.0 - beta_two) * gradient * gradient
    first_hat = first_moment / (1.0 - beta_one**INNER_STEP)
    second_hat = second_moment / (1.0 - beta_two**INNER_STEP)
    inner = params[0] - inner_rate * (
        first_hat / (jnp.sqrt(second_hat) + epsilon) + decay_rate * params[0]
    )
    summed = jnp.sum(to_every(global_params - inner, ISLAND, islands), axis=0)
    delta = summed / islands
    new_mom = momentum * outer_mom + delta
    new_global = global_params - outer_rate * (delta + momentum * new_mom)
    mixed = mixing * inner + (1.0 - mixing) * new_global
    column = to_every(mixed.astype(jnp.bfloat16), "z", Z).reshape(Z * shard_rows, width)
    gathered = to_every(column, PLANE, plane).reshape(padded_rows, width)
    forward_weight = gathered[:features]
    return (
        mixed[None],
        first_moment[None],
        second_moment[None],
        new_global,
        new_mom,
        forward_weight[None],
    )


def solution(mesh):
    grid = Mesh(mesh.devices.reshape(X, Y_LO, Z, Y_HI, CORE), (*FSDP, *ISLAND))
    in_specs = (
        P(ISLAND, FSDP, None),
        P(ISLAND, FSDP, None),
        P(ISLAND, FSDP, None),
        P(ISLAND, FSDP, None),
        P(ISLAND, FSDP, None),
        P(FSDP, None),
        P(FSDP, None),
    )
    out_specs = (
        P(ISLAND, FSDP, None),
        P(ISLAND, FSDP, None),
        P(ISLAND, FSDP, None),
        P(FSDP, None),
        P(FSDP, None),
        P(ISLAND, None, None),
    )
    return jax.shard_map(
        on_device, mesh=grid, in_specs=in_specs, out_specs=out_specs, check_vma=False
    )
```

time: 806 us -> 108 us (0.13)
  waiting for transfers between devices: 470 us -> 12.2 us
  blocking collectives: 280 us -> 78 us
  starting transfers between devices: 26.3 us -> 3.56 us
  between operations: 14.9 us -> 0.77 us
    all_gather x1 -> x0, waiting for transfers between devices: 468 us -> none  [on_device(): lax.all_gather(mixed.astype(jnp.bfloat16), 'fsdp', axis=1, tiled=True)]
    unnamed x1 -> x0, blocking collectives: 256 us -> none
    all_to_all x0 -> x4, blocking collectives: none -> 78 us  [the longest x2 29.9 us: to_every(): return lax.all_to_all(copies, axes, 0, 0)]
    unnamed x10 -> x0, starting transfers between devices: 26.3 us -> none
    psum x1 -> x0, blocking collectives: 24.6 us -> none  [on_device(): summed = lax.psum(global_params[None] - inner, 'island')]
    all_to_all x0 -> x1, waiting for transfers between devices: none -> 12.2 us  [to_every(): return lax.all_to_all(copies, axes, 0, 0)]
  transfers between devices with their start and end apart: 11 -> 1, of which waited for: 2 -> 1; matrix products, arithmetic and copies ran while one was open for 0% -> 2% of each run, Pallas kernels for 0% -> 0%
where the time goes in v1:
time: 108 us
  blocking collectives  78 us (72%)
  waiting for transfers between devices  12.2 us (11%)
  local copies, waits for them, and re-layouts  10.7 us (10%)
  starting transfers between devices  3.56 us (3%)
  matrix products  1.6 us (1%)
    all_to_all x2, blocking collectives, to_every(): return lax.all_to_all(copies, axes, 0, 0)  29.9 us
    all_to_all x1, blocking collectives, on_device(): got = lax.all_to_all(sent, 'z', 0, 0)  26.9 us
    all_to_all x1, blocking collectives, on_device(): got = lax.all_to_all(sent, PLANE, 0, 0)  21.2 us
    all_to_all x1, waiting for transfers between devices, to_every(): return lax.all_to_all(copies, axes, 0, 0)  12.2 us
    all_to_all x1, starting transfers between devices, to_every(): return lax.all_to_all(copies, axes, 0, 0)  3.56 us
    unnamed x17, local copies, waits for them, and re-layouts  3.5 us
    broadcast_in_dim x1, local copies, waits for them, and re-layouts, on_device(): forward_weight[None]  2.26 us
  transfers between devices with their start and end apart: 1, of which 1 were waited for; matrix products, arithmetic and copies ran while one was open for 2% of the time, Pallas kernels for 0%

profile of v1, /device:TPU:16, one launch (start us, length us, event | category | flops | bytes accessed | tf_op | source)
XLA Modules:
  0.0 107.6 jit_solution(10110467799144281671)
XLA Ops:
  0.6 0.0 copy-start
  0.6 1.6 %copy-done = bf16[1,256,4096]{2,1,0:T(8,128)(2,1)S(1)} copy-done((bf16[1,256,4096]{2,1,0:T(8,128)(2,1)S(1)}, bf16[1,256,4096]{2,1,0:T(8,128)(2,1)}, u32[]{:S(2)}) %copy-start) | copy-done | bytes 2097176
  2.2 1.6 %convolution_convert_fusion = f16[4096,128]{1,0:T(8,128)(2,1)S(1)} fusion(bf16[1,256,4096]{2,1,0:T(8,128)(2,1)S(1)} %copy-done, bf16[1,256,128]{2,1,0:T(8,128)(2,1)} %param.8), kind=kOutput, calls=%fused_computation | convolution fusion | flops 268959744 | bytes 3211264 | tf_op jit(solution)/shard_map/td,th->dh/dot_general | solution.py:36
  3.8 1.2 %pad.5 = f16[4128,128]{1,0:T(8,128)(2,1)} pad(f16[4096,128]{1,0:T(8,128)(2,1)S(1)} %convolution_convert_fusion, f16[]{:T(256)} %constant.6.clone.1), padding=0_32x0_0 | pad | bytes 2105346 | tf_op jit(solution)/shard_map/jit(_pad)/pad | solution.py:37
  5.0 1.4 %convert_element_type.21 = f16[8,516,128]{2,1,0:T(8,128)(2,1)S(1)} reshape(f16[4128,128]{1,0:T(8,128)(2,1)} %pad.5) | data formatting | bytes 2113536 | tf_op jit(solution)/shard_map/convert_element_type | solution.py:38
  6.4 21.2 %all_to_all.25 = f16[8,516,128]{2,1,0:T(8,128)(2,1)S(1)} all-to-all(f16[8,516,128]{2,1,0:T(8,128)(2,1)S(1)} %convert_element_type.21), channel_id=1, replica_groups=mesh['x'=4,'y_lo'=2,'z'=12,'y_hi'=4,'core'=2] {'x','y_lo'}, dimensions={0} | all-to-all | bytes 2113536 | tf_op jit(solution)/shard_map/all_to_all | solution.py:39
  27.6 0.0 copy-start.1
  27.6 0.0 copy-start.3
  27.6 0.0 copy-start.4
  27.6 0.0 copy-start.6
  27.7 0.1 convert_reduce_fusion
  27.8 0.0 copy-start.5
  27.8 0.1 convert_element_type.24
  27.9 26.9 %all_to_all.26 = f16[12,43,128]{2,1,0:T(8,128)(2,1)S(1)} all-to-all(f16[12,43,128]{2,1,0:T(8,128)(2,1)S(1)} %convert_element_type.24), channel_id=1, replica_groups=mesh['x'=4,'y_lo'=2,'z'=12,'y_hi'=4,'core'=2] {'z'}, dimensions={0} | all-to-all | bytes 264192 | tf_op jit(solution)/shard_map/all_to_all | solution.py:42
  54.8 0.0 copy-done.1
  54.8 0.0 copy-done.3
  54.8 0.0 copy-done.4
  54.8 0.0 copy-done.6
  54.9 15.2 %all_to_all.27 = f32[8,43,128]{2,1,0:T(8,128)S(1)} all-to-all(f32[8,43,128]{2,1,0:T(8,128)S(1)} %broadcast_in_dim.12), channel_id=1, replica_groups=mesh['x'=4,'y_lo'=2,'z'=12,'y_hi'=4,'core'=2] {'y_hi','core'}, dimensions={0} | all-to-all | bytes 352256 | tf_op jit(solution)/shard_map/all_to_all | solution.py:27
  70.1 0.0 copy-done.5
  70.2 0.6 fusion.11
  70.8 14.7 %all_to_all.28 = bf16[12,43,128]{2,1,0:T(8,128)(2,1)S(1)} all-to-all(bf16[12,43,128]{2,1,0:T(8,128)(2,1)S(1)} %broadcast_in_dim.14), channel_id=1, replica_groups=mesh['x'=4,'y_lo'=2,'z'=12,'y_hi'=4,'core'=2] {'z'}, dimensions={0} | all-to-all | bytes 264192 | tf_op jit(solution)/shard_map/all_to_all | solution.py:27
  85.5 0.1 broadcast_in_dim.30
  85.5 1.1 %broadcast_in_dim.31 = bf16[8,516,128]{2,1,0:T(8,128)(2,1)} broadcast(bf16[516,128]{1,0:T(8,128)(2,1)S(1)} %broadcast_in_dim.30), dimensions={1,2} | broadcast | bytes 1188864 | tf_op jit(solution)/shard_map/broadcast_in_dim | solution.py:26
  86.6 3.6 %all-to-all-start.4 = ((bf16[8,516,128]{2,1,0:T(8,128)(2,1)}), bf16[8,516,128]{2,1,0:T(8,128)(2,1)S(1)}, u32[]{:S(2)}, u32[]{:S(2)}) async-start(bf16[8,516,128]{2,1,0:T(8,128)(2,1)} %broadcast_in_dim.31), calls=%async_computation.4 | async-start | bytes 2129920 | tf_op jit(solution)/shard_map/all_to_all | solution.py:27
  90.2 0.6 copy.30
  90.9 0.6 copy.31
  91.5 0.0 copy-done.2
  91.5 0.6 copy.29
  92.1 12.2 %all-to-all-done.4 = bf16[8,516,128]{2,1,0:T(8,128)(2,1)S(1)} async-done(((bf16[8,516,128]{2,1,0:T(8,128)(2,1)}), bf16[8,516,128]{2,1,0:T(8,128)(2,1)S(1)}, u32[]{:S(2)}, u32[]{:S(2)}) %all-to-all-start.4) | async-done | bytes 1056800 | tf_op jit(solution)/shard_map/all_to_all | solution.py:27
  104.3 1.1 reshape.43
  105.4 2.3 %slice_bitcast_fusion = bf16[1,4096,128]{2,1,0:T(8,128)(2,1)} fusion(bf16[4128,128]{1,0:T(8,128)(2,1)} %reshape.43), kind=kLoop, calls=%fused_computation.3 | loop fusion | bytes 2097152 | tf_op jit(solution)/shard_map/broadcast_in_dim | solution.py:65
  (9 shorter events, 0.2 us)
Async XLA Ops:
  0.6 1.6 %copy-start = (bf16[1,256,4096]{2,1,0:T(8,128)(2,1)S(1)}, bf16[1,256,4096]{2,1,0:T(8,128)(2,1)}, u32[]{:S(2)}) copy-start(bf16[1,256,4096]{2,1,0:T(8,128)(2,1)} %param.7) | copy-start | bytes 6291460
  27.6 27.2 %copy-start.1 = (f32[43,128]{1,0:T(8,128)S(1)}, f32[43,128]{1,0:T(8,128)}, u32[]{:S(2)}) copy-start(f32[43,128]{1,0:T(8,128)} %param.12) | copy-start | bytes 66052
  27.6 27.2 %copy-start.3 = (f32[1,43,128]{2,0,1:T(1,128)S(1)}, f32[1,43,128]{2,0,1:T(1,128)}, u32[]{:S(2)}) copy-start(f32[1,43,128]{2,0,1:T(1,128)} %param.11) | copy-start | bytes 66052
  27.6 27.2 %copy-start.4 = (f32[1,43,128]{2,0,1:T(1,128)S(1)}, f32[1,43,128]{2,0,1:T(1,128)}, u32[]{:S(2)}) copy-start(f32[1,43,128]{2,0,1:T(1,128)} %param.10) | copy-start | bytes 66052
  27.6 27.2 %copy-start.6 = (f32[1,43,128]{2,0,1:T(1,128)S(1)}, f32[1,43,128]{2,0,1:T(1,128)}, u32[]{:S(2)}) copy-start(f32[1,43,128]{2,0,1:T(1,128)} %param.9) | copy-start | bytes 66052
  27.8 42.3 %copy-start.5 = (f32[43,128]{1,0:T(8,128)S(1)}, f32[43,128]{1,0:T(8,128)}, u32[]{:S(2)}) copy-start(f32[43,128]{1,0:T(8,128)} %param.13) | copy-start | bytes 66052
  70.8 20.7 %copy-start.2 = (f32[43,128]{1,0:T(8,128)}, f32[43,128]{1,0:T(8,128)S(1)}, u32[]{:S(2)}) copy-start(f32[43,128]{1,0:T(8,128)S(1)} %get-tuple-element.31) | copy-start | bytes 66052
  86.6 17.6 %all-to-all-start.4 = ((bf16[8,516,128]{2,1,0:T(8,128)(2,1)}), bf16[8,516,128]{2,1,0:T(8,128)(2,1)S(1)}, u32[]{:S(2)}, u32[]{:S(2)}) async-start(bf16[8,516,128]{2,1,0:T(8,128)(2,1)} %broadcast_in_dim.31), calls=%async_computation.4 | async-start | bytes 2129920 | tf_op jit(solution)/shard_map/all_to_all | solution.py:27

commit v2 on v1

--- a/solution.py
+++ b/solution.py
@@ -1,6 +1,9 @@
+import functools
 import jax
 import jax.numpy as jnp
 from jax import lax
+from jax.experimental import pallas as pl
+from jax.experimental.pallas import tpu as pltpu
 from jax.sharding import Mesh
 from jax.sharding import PartitionSpec as P
 
@@ -27,15 +30,119 @@
     return lax.all_to_all(copies, axes, 0, 0)
 
 
+def product_kernel(rows, acts_hbm, cot_hbm, out_ref, acts, cot, whole, arrived, cot_arrived):
+    tokens, features = acts_hbm.shape
+    blocks = out_ref.shape[0]
+    step = features // blocks
+    copies = [
+        pltpu.make_async_copy(
+            acts_hbm.at[:, pl.ds(j * step, step)], acts.at[:, pl.ds(j * step, step)], arrived.at[j]
+        )
+        for j in range(blocks)
+    ]
+    cot_copy = pltpu.make_async_copy(cot_hbm, cot, cot_arrived)
+    cot_copy.start()
+    for copy in copies:
+        copy.start()
+    whole[pl.ds(features, whole.shape[0] - features), :] = jnp.zeros(
+        (whole.shape[0] - features, whole.shape[1]), jnp.float32
+    )
+    cot_copy.wait()
+    for j, copy in enumerate(copies):
+        copy.wait()
+        whole[pl.ds(j * step, step), :] = lax.dot_general(
+            acts[:, pl.ds(j * step, step)],
+            cot[...],
+            (((0,), (0,)), ((), ())),
+            preferred_element_type=jnp.float32,
+        )
+        if j > 0:
+            out_ref[j - 1] = whole[pl.ds((j - 1) * rows, rows), :].astype(out_ref.dtype)
+    out_ref[blocks - 1] = whole[pl.ds((blocks - 1) * rows, rows), :].astype(out_ref.dtype)
+
+
+def product(acts, cot, blocks, rows):
+    tokens, features = acts.shape
+    width = cot.shape[1]
+    return pl.pallas_call(
+        functools.partial(product_kernel, rows),
+        out_shape=jax.ShapeDtypeStruct((blocks, rows, width), jnp.float32),
+        in_specs=[pl.BlockSpec(memory_space=pltpu.HBM)] * 2,
+        out_specs=pl.BlockSpec(memory_space=pltpu.VMEM),
+        scratch_shapes=[
+            pltpu.VMEM((tokens, features), acts.dtype),
+            pltpu.VMEM((tokens, width), cot.dtype),
+            pltpu.VMEM((-(-blocks * rows // 8) * 8, width), jnp.float32),
+            pltpu.SemaphoreType.DMA((blocks,)),
+            pltpu.SemaphoreType.DMA(()),
+        ],
+        compiler_params=pltpu.CompilerParams(vmem_limit_bytes=12 << 20),
+        name="product",
+    )(*(pltpu.with_memory_space_constraint(a, pltpu.HBM) for a in (acts, cot)))
+
+
+def finish_kernel(rows, tall, *refs):
+    small = (len(refs) - 5) // 2
+    blocks_ref, arrays, out_hbm = refs[0], refs[1 : small + 1], refs[small + 1]
+    outs = refs[small + 2 : 2 * small + 2]
+    joined, upright, left = refs[2 * small + 2 :]
+    blocks = blocks_ref.shape[0]
+    step = out_hbm.shape[0] // blocks
+    copies = []
+
+    def send(source, target):
+        copies.append(pltpu.make_async_copy(source, target, left.at[len(copies)]))
+        copies[-1].start()
+
+    for j in range(blocks):
+        first = j * step
+        while first < (j + 1) * step:
+            b = first // rows
+            last = min((j + 1) * step, (b + 1) * rows)
+            joined[pl.ds(first, last - first), :] = blocks_ref[b, pl.ds(first - b * rows, last - first), :]
+            first = last
+        send(joined.at[pl.ds(j * step, step)], out_hbm.at[pl.ds(j * step, step)])
+    for i in range(small):
+        if i < tall:
+            upright[i, :, 0, :] = arrays[i][...]
+            send(upright.at[i], outs[i])
+        else:
+            send(arrays[i], outs[i])
+    for copy in copies:
+        copy.wait()
+
+
+def finish(blocks, features, tall, flat):
+    count, rows, width = blocks.shape
+    shard_rows = tall[0].shape[0]
+    arrays = (*tall, *flat)
+    f32 = jnp.float32
+    out = pl.pallas_call(
+        functools.partial(finish_kernel, rows, len(tall)),
+        out_shape=[
+            jax.ShapeDtypeStruct((features, width), blocks.dtype),
+            *[jax.ShapeDtypeStruct((shard_rows, 1, width), f32) for _ in tall],
+            *[jax.ShapeDtypeStruct((shard_rows, width), f32) for _ in flat],
+        ],
+        in_specs=[pl.BlockSpec(memory_space=pltpu.VMEM)] * (1 + len(arrays)),
+        out_specs=[pl.BlockSpec(memory_space=pltpu.HBM)] * (1 + len(arrays)),
+        scratch_shapes=[
+            pltpu.VMEM((features, width), blocks.dtype),
+            pltpu.VMEM((len(tall), shard_rows, 1, width), f32),
+            pltpu.SemaphoreType.DMA((count + len(arrays),)),
+        ],
+        compiler_params=pltpu.CompilerParams(vmem_limit_bytes=4 << 20),
+        name="finish",
+    )(blocks, *arrays)
+    return out[0], [jnp.swapaxes(a, 0, 1) for a in out[1 : 1 + len(tall)]], out[1 + len(tall) :]
+
+
 def on_device(acts, grad_out, params, adam_m, adam_v, global_params, outer_mom):
     shard_rows = params.shape[1]
     features = acts.shape[2]
     width = params.shape[2]
     plane, islands = X * Y_LO, Y_HI * CORE
-    padded_rows = shard_rows * plane * Z
-    whole = jnp.einsum("td,th->dh", acts[0], grad_out[0], preferred_element_type=jnp.float32)
-    whole = jnp.pad(whole, ((0, padded_rows - features), (0, 0)))
-    sent = whole.reshape(plane, Z * shard_rows, width).astype(jnp.float16)
+    sent = product(acts[0], grad_out[0], plane, Z * shard_rows).astype(jnp.float16)
     got = lax.all_to_all(sent, PLANE, 0, 0)
     part = jnp.sum(got.astype(jnp.float32), axis=0)
     sent = part.reshape(Z, shard_rows, width).astype(jnp.float16)
@@ -54,16 +161,13 @@
     new_global = global_params - outer_rate * (delta + momentum * new_mom)
     mixed = mixing * inner + (1.0 - mixing) * new_global
     column = to_every(mixed.astype(jnp.bfloat16), "z", Z).reshape(Z * shard_rows, width)
-    gathered = to_every(column, PLANE, plane).reshape(padded_rows, width)
-    forward_weight = gathered[:features]
-    return (
-        mixed[None],
-        first_moment[None],
-        second_moment[None],
-        new_global,
-        new_mom,
-        forward_weight[None],
+    forward_weight, tall, flat = finish(
+        to_every(column, PLANE, plane),
+        features,
+        (mixed, first_moment, second_moment),
+        (new_global, new_mom),
     )
+    return (*tall, *flat, forward_weight[None])
 
 
 def solution(mesh):

time: 108 us -> 103 us (0.954)
  blocking collectives: 78 us -> 95.6 us
  waiting for transfers between devices: 12.2 us -> 0 us
  local copies, waits for them, and re-layouts: 10.7 us -> 0.31 us
  Pallas kernels: 0 us -> 5.23 us
  starting transfers between devices: 3.56 us -> 0 us
  matrix products: 1.6 us -> 0 us
    all_to_all x2 -> x3, blocking collectives: 29.9 us -> 47.5 us  [to_every(): return lax.all_to_all(copies, axes, 0, 0)]
    all_to_all x1 -> x0, waiting for transfers between devices: 12.2 us -> none  [to_every(): return lax.all_to_all(copies, axes, 0, 0)]
    pallas_call x0 -> x2, Pallas kernels: none -> 5.23 us  [the longest x1 4.13 us: product(): pl.pallas_call(functools.partial(product_kernel, rows), out_shape=jax.Sha...]
    all_to_all x1 -> x0, starting transfers between devices: 3.56 us -> none  [to_every(): return lax.all_to_all(copies, axes, 0, 0)]
    unnamed x17 -> x10, local copies, waits for them, and re-layouts: 3.5 us -> 0.02 us
    broadcast_in_dim x1 -> x0, local copies, waits for them, and re-layouts: 2.26 us -> none  [on_device(): forward_weight[None]]
    dot_general x1 -> x0, matrix products: 1.6 us -> none  [on_device(): jnp.einsum('td,th->dh', acts[0], grad_out[0], preferred_element_type=jnp....]
    convert_element_type x1 -> x0, local copies, waits for them, and re-layouts: 1.38 us -> none  [on_device(): sent = whole.reshape(plane, Z * shard_rows, width).astype(jnp.float16)]
  transfers between devices with their start and end apart: 1 -> 0, of which waited for: 1 -> 0; matrix products, arithmetic and copies ran while one was open for 2% -> 0% of each run, Pallas kernels for 0% -> 0%
where the time goes in v2:
time: 103 us; the launch traced here: 102 us
  blocking collectives  95.6 us (93%)
  Pallas kernels  5.23 us (5%)
    all_to_all x3, blocking collectives, to_every(): return lax.all_to_all(copies, axes, 0, 0)  47.5 us
    all_to_all x1, blocking collectives, on_device(): got = lax.all_to_all(sent, 'z', 0, 0)  26.9 us
    all_to_all x1, blocking collectives, on_device(): got = lax.all_to_all(sent, PLANE, 0, 0)  21.2 us
    pallas_call x1, Pallas kernels, product(): pl.pallas_call(functools.partial(product_kernel, rows), out_shape=jax.Sha...  4.13 us

profile of v2, /device:TPU:16, one launch (start us, length us, event | category | flops | bytes accessed | tf_op | source)
XLA Modules:
  0.0 102.3 jit_solution(8125974812400881678)
XLA Ops:
  0.6 4.1 %product.1 = f32[8,516,128]{2,1,0:T(8,128)S(1)} custom-call(bf16[256,4096]{1,0:T(8,128)(2,1)} %bitcast.26, bf16[256,128]{1,0:T(8,128)(2,1)} %bitcast.27), custom_call_target="tpu_custom_call" | custom-call | tf_op jit(solution)/shard_map/product/pallas_call | solution.py:67
  4.8 0.1 convert_element_type.18
  4.9 21.2 %all_to_all.25 = f16[8,516,128]{2,1,0:T(8,128)(2,1)S(1)} all-to-all(f16[8,516,128]{2,1,0:T(8,128)(2,1)S(1)} %convert_element_type.18), channel_id=1, replica_groups=mesh['x'=4,'y_lo'=2,'z'=12,'y_hi'=4,'core'=2] {'x','y_lo'}, dimensions={0} | all-to-all | bytes 2113536 | tf_op jit(solution)/shard_map/all_to_all | solution.py:146
  26.1 0.0 copy-start
  26.2 0.0 copy-start.1
  26.2 0.0 copy-start.3
  26.2 0.0 copy-start.4
  26.2 0.1 convert_reduce_fusion
  26.3 0.0 copy-start.2
  26.3 0.1 convert_element_type.21
  26.4 26.9 %all_to_all.26 = f16[12,43,128]{2,1,0:T(8,128)(2,1)S(1)} all-to-all(f16[12,43,128]{2,1,0:T(8,128)(2,1)S(1)} %convert_element_type.21), channel_id=1, replica_groups=mesh['x'=4,'y_lo'=2,'z'=12,'y_hi'=4,'core'=2] {'z'}, dimensions={0} | all-to-all | bytes 264192 | tf_op jit(solution)/shard_map/all_to_all | solution.py:149
  53.3 0.0 copy-done
  53.3 0.0 copy-done.1
  53.3 0.0 copy-done.3
  53.3 0.0 copy-done.4
  53.4 15.2 %all_to_all.27 = f32[8,43,128]{2,1,0:T(8,128)S(1)} all-to-all(f32[8,43,128]{2,1,0:T(8,128)S(1)} %broadcast_in_dim.10), channel_id=1, replica_groups=mesh['x'=4,'y_lo'=2,'z'=12,'y_hi'=4,'core'=2] {'y_hi','core'}, dimensions={0} | all-to-all | bytes 352256 | tf_op jit(solution)/shard_map/all_to_all | solution.py:30
  68.7 0.0 copy-done.2
  68.7 14.7 %all_to_all.28 = bf16[12,43,128]{2,1,0:T(8,128)(2,1)S(1)} all-to-all(bf16[12,43,128]{2,1,0:T(8,128)(2,1)S(1)} %broadcast_in_dim.11), channel_id=1, replica_groups=mesh['x'=4,'y_lo'=2,'z'=12,'y_hi'=4,'core'=2] {'z'}, dimensions={0} | all-to-all | bytes 264192 | tf_op jit(solution)/shard_map/all_to_all | solution.py:30
  83.4 0.1 broadcast_in_dim.24
  83.5 0.1 broadcast_in_dim.25
  83.6 17.6 %all_to_all.29.refs_0_ = bf16[8,516,128]{2,1,0:T(8,128)(2,1)S(1)} all-to-all(bf16[8,516,128]{2,1,0:T(8,128)(2,1)S(1)} %broadcast_in_dim.25), channel_id=1, replica_groups=mesh['x'=4,'y_lo'=2,'z'=12,'y_hi'=4,'core'=2] {'x','y_lo'}, dimensions={0} | all-to-all | bytes 2113536 | tf_op jit(solution)/shard_map/all_to_all | solution.py:30
  101.2 1.1 %finish.1 = (bf16[4096,128]{1,0:T(8,128)(2,1)}, f32[43,1,128]{2,1,0:T(1,128)}, f32[43,1,128]{2,1,0:T(1,128)}, f32[43,1,128]{2,1,0:T(1,128)}, f32[43,128]{1,0:T(8,128)}, /*index=5*/f32[43,128]{1,0:T(8,128)}) custom-call(bf16[8,516,128]{2,1,0:T(8,128)(2,1)S(1)} %all_to_all.29.refs_0_, f32[43,128]{1,0:T(8,128)S(1)} %get-tuple-element.19.refs_1_, ...), custom_call_target="tpu_custom_call" | custom-call | tf_op jit(solution)/shard_map/finish/pallas_call | solution.py:120
  (7 shorter events, 0.2 us)
Async XLA Ops:
  26.1 27.2 %copy-start = (f32[43,128]{1,0:T(8,128)S(1)}, f32[43,128]{1,0:T(8,128)}, u32[]{:S(2)}) copy-start(f32[43,128]{1,0:T(8,128)} %param.12) | copy-start | bytes 66052
  26.2 27.2 %copy-start.1 = (f32[1,43,128]{2,0,1:T(1,128)S(1)}, f32[1,43,128]{2,0,1:T(1,128)}, u32[]{:S(2)}) copy-start(f32[1,43,128]{2,0,1:T(1,128)} %param.9) | copy-start | bytes 66052
  26.2 27.2 %copy-start.3 = (f32[1,43,128]{2,0,1:T(1,128)S(1)}, f32[1,43,128]{2,0,1:T(1,128)}, u32[]{:S(2)}) copy-start(f32[1,43,128]{2,0,1:T(1,128)} %param.10) | copy-start | bytes 66052
  26.2 27.2 %copy-start.4 = (f32[1,43,128]{2,0,1:T(1,128)S(1)}, f32[1,43,128]{2,0,1:T(1,128)}, u32[]{:S(2)}) copy-start(f32[1,43,128]{2,0,1:T(1,128)} %param.11) | copy-start | bytes 66052
  26.3 42.3 %copy-start.2 = (f32[43,128]{1,0:T(8,128)S(1)}, f32[43,128]{1,0:T(8,128)}, u32[]{:S(2)}) copy-start(f32[43,128]{1,0:T(8,128)} %param.13) | copy-start | bytes 66052

commit v3 on v2

--- a/solution.py
+++ b/solution.py
@@ -20,6 +20,7 @@
 mixing = 0.5
 
 X, Y_LO, Z, Y_HI, CORE = 4, 2, 12, 4, 2
+STEPS = 2
 PLANE = ("x", "y_lo")
 FSDP = ("x", "y_lo", "z")
 ISLAND = ("y_hi", "core")
@@ -30,53 +31,56 @@
     return lax.all_to_all(copies, axes, 0, 0)
 
 
-def product_kernel(rows, acts_hbm, cot_hbm, out_ref, acts, cot, whole, arrived, cot_arrived):
-    tokens, features = acts_hbm.shape
-    blocks = out_ref.shape[0]
-    step = features // blocks
+def product_kernel(acts_hbm, cot_hbm, out_ref, acts, cot, arrived, cot_arrived):
+    features = acts_hbm.shape[1]
+    blocks, rows, width = out_ref.shape
+    step = features // STEPS
+    cot_copy = pltpu.make_async_copy(cot_hbm, cot, cot_arrived)
+    cot_copy.start()
     copies = [
         pltpu.make_async_copy(
             acts_hbm.at[:, pl.ds(j * step, step)], acts.at[:, pl.ds(j * step, step)], arrived.at[j]
         )
-        for j in range(blocks)
+        for j in range(STEPS)
     ]
-    cot_copy = pltpu.make_async_copy(cot_hbm, cot, cot_arrived)
-    cot_copy.start()
     for copy in copies:
         copy.start()
-    whole[pl.ds(features, whole.shape[0] - features), :] = jnp.zeros(
-        (whole.shape[0] - features, whole.shape[1]), jnp.float32
-    )
+    past = features - (blocks - 1) * rows
+    out_ref[blocks - 1, pl.ds(past, rows - past), :] = jnp.zeros((rows - past, width), jnp.float32)
     cot_copy.wait()
     for j, copy in enumerate(copies):
         copy.wait()
-        whole[pl.ds(j * step, step), :] = lax.dot_general(
+        part = lax.dot_general(
+            cot[...],
             acts[:, pl.ds(j * step, step)],
-            cot[...],
             (((0,), (0,)), ((), ())),
             preferred_element_type=jnp.float32,
-        )
-        if j > 0:
-            out_ref[j - 1] = whole[pl.ds((j - 1) * rows, rows), :].astype(out_ref.dtype)
-    out_ref[blocks - 1] = whole[pl.ds((blocks - 1) * rows, rows), :].astype(out_ref.dtype)
+        ).T
+        first = j * step
+        while first < (j + 1) * step:
+            b = first // rows
+            last = min((b + 1) * rows, (j + 1) * step)
+            if first % 8:
+                last = min(last, -(-first // 8) * 8)
+            out_ref[b, pl.ds(first - b * rows, last - first), :] = part[first - j * step : last - j * step]
+            first = last
 
 
 def product(acts, cot, blocks, rows):
     tokens, features = acts.shape
     width = cot.shape[1]
     return pl.pallas_call(
-        functools.partial(product_kernel, rows),
+        product_kernel,
         out_shape=jax.ShapeDtypeStruct((blocks, rows, width), jnp.float32),
         in_specs=[pl.BlockSpec(memory_space=pltpu.HBM)] * 2,
         out_specs=pl.BlockSpec(memory_space=pltpu.VMEM),
         scratch_shapes=[
             pltpu.VMEM((tokens, features), acts.dtype),
             pltpu.VMEM((tokens, width), cot.dtype),
-            pltpu.VMEM((-(-blocks * rows // 8) * 8, width), jnp.float32),
-            pltpu.SemaphoreType.DMA((blocks,)),
+            pltpu.SemaphoreType.DMA((STEPS,)),
             pltpu.SemaphoreType.DMA(()),
         ],
-        compiler_params=pltpu.CompilerParams(vmem_limit_bytes=12 << 20),
+        compiler_params=pltpu.CompilerParams(vmem_limit_bytes=8 << 20),
         name="product",
     )(*(pltpu.with_memory_space_constraint(a, pltpu.HBM) for a in (acts, cot)))
 

time: 103 us -> 101 us (0.981)
  Pallas kernels: 5.23 us -> 3.43 us
    pallas_call x1, Pallas kernels: 4.13 us -> 2.33 us  [product(): pl.pallas_call(product_kernel, out_shape=jax.ShapeDtypeStruct((blocks, ro...]
where the time goes in v3:
time: 101 us
  blocking collectives  95.6 us (95%)
  Pallas kernels  3.43 us (3%)
    all_to_all x3, blocking collectives, to_every(): return lax.all_to_all(copies, axes, 0, 0)  47.5 us
    all_to_all x1, blocking collectives, on_device(): got = lax.all_to_all(sent, 'z', 0, 0)  26.9 us
    all_to_all x1, blocking collectives, on_device(): got = lax.all_to_all(sent, PLANE, 0, 0)  21.2 us
    pallas_call x1, Pallas kernels, product(): pl.pallas_call(product_kernel, out_shape=jax.ShapeDtypeStruct((blocks, ro...  2.33 us

profile of v3, /device:TPU:16, one launch (start us, length us, event | category | flops | bytes accessed | tf_op | source)
XLA Modules:
  0.0 100.5 jit_solution(2117287017268599533)
XLA Ops:
  0.6 2.3 %product.1 = f32[8,516,128]{2,1,0:T(8,128)S(1)} custom-call(bf16[256,4096]{1,0:T(8,128)(2,1)} %bitcast.26, bf16[256,128]{1,0:T(8,128)(2,1)} %bitcast.27), custom_call_target="tpu_custom_call" | custom-call | tf_op jit(solution)/shard_map/product/pallas_call | solution.py:72
  3.0 0.1 convert_element_type.18
  3.1 21.2 %all_to_all.25 = f16[8,516,128]{2,1,0:T(8,128)(2,1)S(1)} all-to-all(f16[8,516,128]{2,1,0:T(8,128)(2,1)S(1)} %convert_element_type.18), channel_id=1, replica_groups=mesh['x'=4,'y_lo'=2,'z'=12,'y_hi'=4,'core'=2] {'x','y_lo'}, dimensions={0} | all-to-all | bytes 2113536 | tf_op jit(solution)/shard_map/all_to_all | solution.py:150
  24.3 0.0 copy-start
  24.3 0.0 copy-start.1
  24.4 0.0 copy-start.3
  24.4 0.0 copy-start.4
  24.4 0.1 convert_reduce_fusion
  24.5 0.0 copy-start.2
  24.5 0.1 convert_element_type.21
  24.6 26.9 %all_to_all.26 = f16[12,43,128]{2,1,0:T(8,128)(2,1)S(1)} all-to-all(f16[12,43,128]{2,1,0:T(8,128)(2,1)S(1)} %convert_element_type.21), channel_id=1, replica_groups=mesh['x'=4,'y_lo'=2,'z'=12,'y_hi'=4,'core'=2] {'z'}, dimensions={0} | all-to-all | bytes 264192 | tf_op jit(solution)/shard_map/all_to_all | solution.py:153
  51.5 0.0 copy-done
  51.5 0.0 copy-done.1
  51.5 0.0 copy-done.3
  51.5 0.0 copy-done.4
  51.6 15.2 %all_to_all.27 = f32[8,43,128]{2,1,0:T(8,128)S(1)} all-to-all(f32[8,43,128]{2,1,0:T(8,128)S(1)} %broadcast_in_dim.10), channel_id=1, replica_groups=mesh['x'=4,'y_lo'=2,'z'=12,'y_hi'=4,'core'=2] {'y_hi','core'}, dimensions={0} | all-to-all | bytes 352256 | tf_op jit(solution)/shard_map/all_to_all | solution.py:31
  66.9 0.0 copy-done.2
  66.9 14.7 %all_to_all.28 = bf16[12,43,128]{2,1,0:T(8,128)(2,1)S(1)} all-to-all(bf16[12,43,128]{2,1,0:T(8,128)(2,1)S(1)} %broadcast_in_dim.11), channel_id=1, replica_groups=mesh['x'=4,'y_lo'=2,'z'=12,'y_hi'=4,'core'=2] {'z'}, dimensions={0} | all-to-all | bytes 264192 | tf_op jit(solution)/shard_map/all_to_all | solution.py:31
  81.6 0.1 broadcast_in_dim.24
  81.7 0.1 broadcast_in_dim.25
  81.8 17.6 %all_to_all.29.refs_0_ = bf16[8,516,128]{2,1,0:T(8,128)(2,1)S(1)} all-to-all(bf16[8,516,128]{2,1,0:T(8,128)(2,1)S(1)} %broadcast_in_dim.25), channel_id=1, replica_groups=mesh['x'=4,'y_lo'=2,'z'=12,'y_hi'=4,'core'=2] {'x','y_lo'}, dimensions={0} | all-to-all | bytes 2113536 | tf_op jit(solution)/shard_map/all_to_all | solution.py:31
  99.4 1.1 %finish.1 = (bf16[4096,128]{1,0:T(8,128)(2,1)}, f32[43,1,128]{2,1,0:T(1,128)}, f32[43,1,128]{2,1,0:T(1,128)}, f32[43,1,128]{2,1,0:T(1,128)}, f32[43,128]{1,0:T(8,128)}, /*index=5*/f32[43,128]{1,0:T(8,128)}) custom-call(bf16[8,516,128]{2,1,0:T(8,128)(2,1)S(1)} %all_to_all.29.refs_0_, f32[43,128]{1,0:T(8,128)S(1)} %get-tuple-element.19.refs_1_, ...), custom_call_target="tpu_custom_call" | custom-call | tf_op jit(solution)/shard_map/finish/pallas_call | solution.py:124
  (7 shorter events, 0.2 us)
Async XLA Ops:
  24.3 27.2 %copy-start = (f32[43,128]{1,0:T(8,128)S(1)}, f32[43,128]{1,0:T(8,128)}, u32[]{:S(2)}) copy-start(f32[43,128]{1,0:T(8,128)} %param.12) | copy-start | bytes 66052
  24.3 27.2 %copy-start.1 = (f32[1,43,128]{2,0,1:T(1,128)S(1)}, f32[1,43,128]{2,0,1:T(1,128)}, u32[]{:S(2)}) copy-start(f32[1,43,128]{2,0,1:T(1,128)} %param.9) | copy-start | bytes 66052
  24.4 27.2 %copy-start.3 = (f32[1,43,128]{2,0,1:T(1,128)S(1)}, f32[1,43,128]{2,0,1:T(1,128)}, u32[]{:S(2)}) copy-start(f32[1,43,128]{2,0,1:T(1,128)} %param.10) | copy-start | bytes 66052
  24.4 27.2 %copy-start.4 = (f32[1,43,128]{2,0,1:T(1,128)S(1)}, f32[1,43,128]{2,0,1:T(1,128)}, u32[]{:S(2)}) copy-start(f32[1,43,128]{2,0,1:T(1,128)} %param.11) | copy-start | bytes 66052
  24.5 42.4 %copy-start.2 = (f32[43,128]{1,0:T(8,128)S(1)}, f32[43,128]{1,0:T(8,128)}, u32[]{:S(2)}) copy-start(f32[43,128]{1,0:T(8,128)} %param.13) | copy-start | bytes 66052

commit v4 on v3

--- a/solution.py
+++ b/solution.py
@@ -19,16 +19,20 @@
 momentum = 0.9
 mixing = 0.5
 
-X, Y_LO, Z, Y_HI, CORE = 4, 2, 12, 4, 2
+X, Y_LO, Z = 4, 2, 12
 STEPS = 2
-PLANE = ("x", "y_lo")
-FSDP = ("x", "y_lo", "z")
-ISLAND = ("y_hi", "core")
-
-
-def to_every(block, axes, count):
-    copies = jnp.broadcast_to(block[None], (count, *block.shape))
-    return lax.all_to_all(copies, axes, 0, 0)
+PLANE = X * Y_LO
+FSDP = ("plane", "z")
+
+
+def exchange(blocks, axis, turned=False):
+    members = list(range(blocks.shape[0]))
+    groups = [members[::-1]] if turned else None
+    return lax.all_to_all(blocks, axis, 0, 0, axis_index_groups=groups)
+
+
+def copies_of(block, count):
+    return jnp.broadcast_to(block[None], (count, *block.shape))
 
 
 def product_kernel(acts_hbm, cot_hbm, out_ref, acts, cot, arrived, cot_arrived):
@@ -145,12 +149,12 @@
     shard_rows = params.shape[1]
     features = acts.shape[2]
     width = params.shape[2]
-    plane, islands = X * Y_LO, Y_HI * CORE
-    sent = product(acts[0], grad_out[0], plane, Z * shard_rows).astype(jnp.float16)
-    got = lax.all_to_all(sent, PLANE, 0, 0)
+    islands = lax.axis_size("island")
+    sent = product(acts[0], grad_out[0], PLANE, Z * shard_rows).astype(jnp.float16)
+    got = exchange(sent, "plane")
     part = jnp.sum(got.astype(jnp.float32), axis=0)
     sent = part.reshape(Z, shard_rows, width).astype(jnp.float16)
-    got = lax.all_to_all(sent, "z", 0, 0)
+    got = exchange(sent[::-1], "z", turned=True)
     gradient = jnp.sum(got.astype(jnp.float32), axis=0)
     first_moment = beta_one * adam_m[0] + (1.0 - beta_one) * gradient
     second_moment = beta_two * adam_v[0] + (1.0 - beta_two) * gradient * gradient
@@ -159,14 +163,15 @@
     inner = params[0] - inner_rate * (
         first_hat / (jnp.sqrt(second_hat) + epsilon) + decay_rate * params[0]
     )
-    summed = jnp.sum(to_every(global_params - inner, ISLAND, islands), axis=0)
+    summed = jnp.sum(exchange(copies_of(global_params - inner, islands), "island", turned=True)[::-1], axis=0)
     delta = summed / islands
     new_mom = momentum * outer_mom + delta
     new_global = global_params - outer_rate * (delta + momentum * new_mom)
     mixed = mixing * inner + (1.0 - mixing) * new_global
-    column = to_every(mixed.astype(jnp.bfloat16), "z", Z).reshape(Z * shard_rows, width)
+    column = exchange(copies_of(mixed.astype(jnp.bfloat16), Z), "z", turned=True)[::-1]
+    column = column.reshape(Z * shard_rows, width)
     forward_weight, tall, flat = finish(
-        to_every(column, PLANE, plane),
+        exchange(copies_of(column, PLANE), "plane"),
         features,
         (mixed, first_moment, second_moment),
         (new_global, new_mom),
@@ -175,23 +180,23 @@
 
 
 def solution(mesh):
-    grid = Mesh(mesh.devices.reshape(X, Y_LO, Z, Y_HI, CORE), (*FSDP, *ISLAND))
+    grid = Mesh(mesh.devices.reshape(PLANE, Z, -1), (*FSDP, "island"))
     in_specs = (
-        P(ISLAND, FSDP, None),
-        P(ISLAND, FSDP, None),
-        P(ISLAND, FSDP, None),
-        P(ISLAND, FSDP, None),
-        P(ISLAND, FSDP, None),
+        P("island", FSDP, None),
+        P("island", FSDP, None),
+        P("island", FSDP, None),
+        P("island", FSDP, None),
+        P("island", FSDP, None),
         P(FSDP, None),
         P(FSDP, None),
     )
     out_specs = (
-        P(ISLAND, FSDP, None),
-        P(ISLAND, FSDP, None),
-        P(ISLAND, FSDP, None),
-        P(FSDP, None),
-        P(FSDP, None),
-        P(ISLAND, None, None),
+        P("island", FSDP, None),
+        P("island", FSDP, None),
+        P("island", FSDP, None),
+        P(FSDP, None),
+        P(FSDP, None),
+        P("island", None, None),
     )
     return jax.shard_map(
         on_device, mesh=grid, in_specs=in_specs, out_specs=out_specs, check_vma=False

time: 101 us -> 97.1 us (0.961)
  blocking collectives: 95.6 us -> 91.7 us
    all_to_all x5, blocking collectives: 95.6 us -> 91.7 us  [exchange(): return lax.all_to_all(blocks, axis, 0, 0, axis_index_groups=groups)]
where the time goes in v4:
time: 97.1 us; the launch traced here: 96.7 us
  blocking collectives  91.7 us (94%)
  Pallas kernels  3.43 us (4%)
    all_to_all x5, blocking collectives, exchange(): return lax.all_to_all(blocks, axis, 0, 0, axis_index_groups=groups)  91.7 us
    pallas_call x1, Pallas kernels, product(): pl.pallas_call(product_kernel, out_shape=jax.ShapeDtypeStruct((blocks, ro...  2.33 us

profile of v4, /device:TPU:16, one launch (start us, length us, event | category | flops | bytes accessed | tf_op | source)
XLA Modules:
  0.0 96.7 jit_solution(14936306793229311468)
XLA Ops:
  0.6 2.3 %product.1 = f32[8,516,128]{2,1,0:T(8,128)S(1)} custom-call(bf16[256,4096]{1,0:T(8,128)(2,1)} %bitcast.26, bf16[256,128]{1,0:T(8,128)(2,1)} %bitcast.27), custom_call_target="tpu_custom_call" | custom-call | tf_op jit(solution)/shard_map/product/pallas_call | solution.py:76
  3.0 0.1 convert_element_type.18
  3.1 21.2 %all_to_all.25 = f16[8,516,128]{2,1,0:T(8,128)(2,1)S(1)} all-to-all(f16[8,516,128]{2,1,0:T(8,128)(2,1)S(1)} %convert_element_type.18), channel_id=1, replica_groups=mesh['plane'=8,'z'=12,'island'=8] {'plane'}, dimensions={0} | all-to-all | bytes 2113536 | tf_op jit(solution)/shard_map/all_to_all | solution.py:31
  24.3 0.0 copy-start
  24.3 0.0 copy-start.1
  24.4 0.0 copy-start.3
  24.4 0.0 copy-start.4
  24.4 0.1 convert_reduce_fusion
  24.5 0.0 copy-start.2
  24.5 0.1 convert_element_type.21
  24.7 25.7 %all_to_all.26 = f16[12,43,128]{2,1,0:T(8,128)(2,1)S(1)} all-to-all(f16[12,43,128]{2,1,0:T(8,128)(2,1)S(1)} %rev.9), channel_id=1, replica_groups={{88,80,72,64,56,48,40,32,24,16,8,0},{89,81,73,65,57,49,41,33,25,17,9,1}..., dimensions={0} | all-to-all | bytes 264192 | tf_op jit(solution)/shard_map/all_to_all | solution.py:31
  50.4 0.0 copy-done
  50.4 0.0 copy-done.1
  50.4 0.0 copy-done.3
  50.4 0.0 copy-done.4
  50.5 12.0 %all_to_all.27 = f32[8,43,128]{2,1,0:T(8,128)S(1)} all-to-all(f32[8,43,128]{2,1,0:T(8,128)S(1)} %broadcast_in_dim.10), channel_id=1, replica_groups={{7,6,5,4,3,2,1,0},{15,14,13,12,11,10,9,8},{23,22,21,20,19,18,17,16},{31..., dimensions={0} | all-to-all | bytes 352256 | tf_op jit(solution)/shard_map/all_to_all | solution.py:31
  62.5 0.0 copy-done.2
  62.6 15.6 %all_to_all.28 = bf16[12,43,128]{2,1,0:T(8,128)(2,1)S(1)} all-to-all(bf16[12,43,128]{2,1,0:T(8,128)(2,1)S(1)} %broadcast_in_dim.11), channel_id=1, replica_groups={{88,80,72,64,56,48,40,32,24,16,8,0},{89,81,73,65,57,49,41,33,25,17,9,1}..., dimensions={0} | all-to-all | bytes 264192 | tf_op jit(solution)/shard_map/all_to_all | solution.py:31
  78.2 0.1 broadcast_in_dim.24
  78.3 0.1 broadcast_in_dim.25
  78.4 17.2 %all_to_all.29.refs_0_ = bf16[8,516,128]{2,1,0:T(8,128)(2,1)S(1)} all-to-all(bf16[8,516,128]{2,1,0:T(8,128)(2,1)S(1)} %broadcast_in_dim.25), channel_id=1, replica_groups=mesh['plane'=8,'z'=12,'island'=8] {'plane'}, dimensions={0} | all-to-all | bytes 2113536 | tf_op jit(solution)/shard_map/all_to_all | solution.py:31
  95.6 1.1 %finish.1 = (bf16[4096,128]{1,0:T(8,128)(2,1)}, f32[43,1,128]{2,1,0:T(1,128)}, f32[43,1,128]{2,1,0:T(1,128)}, f32[43,1,128]{2,1,0:T(1,128)}, f32[43,128]{1,0:T(8,128)}, /*index=5*/f32[43,128]{1,0:T(8,128)}) custom-call(bf16[8,516,128]{2,1,0:T(8,128)(2,1)S(1)} %all_to_all.29.refs_0_, f32[43,128]{1,0:T(8,128)S(1)} %get-tuple-element.19.refs_1_, ...), custom_call_target="tpu_custom_call" | custom-call | tf_op jit(solution)/shard_map/finish/pallas_call | solution.py:128
  (9 shorter events, 0.2 us)
Async XLA Ops:
  24.3 26.0 %copy-start = (f32[43,128]{1,0:T(8,128)S(1)}, f32[43,128]{1,0:T(8,128)}, u32[]{:S(2)}) copy-start(f32[43,128]{1,0:T(8,128)} %param.12) | copy-start | bytes 66052
  24.3 26.1 %copy-start.1 = (f32[1,43,128]{2,0,1:T(1,128)S(1)}, f32[1,43,128]{2,0,1:T(1,128)}, u32[]{:S(2)}) copy-start(f32[1,43,128]{2,0,1:T(1,128)} %param.9) | copy-start | bytes 66052
  24.4 26.1 %copy-start.3 = (f32[1,43,128]{2,0,1:T(1,128)S(1)}, f32[1,43,128]{2,0,1:T(1,128)}, u32[]{:S(2)}) copy-start(f32[1,43,128]{2,0,1:T(1,128)} %param.10) | copy-start | bytes 66052
  24.4 26.1 %copy-start.4 = (f32[1,43,128]{2,0,1:T(1,128)S(1)}, f32[1,43,128]{2,0,1:T(1,128)}, u32[]{:S(2)}) copy-start(f32[1,43,128]{2,0,1:T(1,128)} %param.11) | copy-start | bytes 66052
  24.5 38.0 %copy-start.2 = (f32[43,128]{1,0:T(8,128)S(1)}, f32[43,128]{1,0:T(8,128)}, u32[]{:S(2)}) copy-start(f32[43,128]{1,0:T(8,128)} %param.13) | copy-start | bytes 66052

commit v5 on v4

--- a/solution.py
+++ b/solution.py
@@ -29,6 +29,22 @@
     members = list(range(blocks.shape[0]))
     groups = [members[::-1]] if turned else None
     return lax.all_to_all(blocks, axis, 0, 0, axis_index_groups=groups)
+
+
+def exchange_z(listed):
+    half = Z // 2
+    groups = [[z for near in range(half) for z in (Z - 1 - near, half - 1 - near)]]
+    return lax.all_to_all(listed, "z", 0, 0, axis_index_groups=groups)
+
+
+def listed_z(blocks):
+    shape = blocks.shape[1:]
+    return jnp.swapaxes(blocks[::-1].reshape(2, Z // 2, *shape), 0, 1).reshape(Z, *shape)
+
+
+def unlisted_z(listed):
+    shape = listed.shape[1:]
+    return jnp.swapaxes(listed.reshape(Z // 2, 2, *shape), 0, 1).reshape(Z, *shape)[::-1]
 
 
 def copies_of(block, count):
@@ -107,7 +123,7 @@
         while first < (j + 1) * step:
             b = first // rows
             last = min((j + 1) * step, (b + 1) * rows)
-            joined[pl.ds(first, last - first), :] = blocks_ref[b, pl.ds(first - b * rows, last - first), :]
+            joined[pl.ds(first, last - first), :] = blocks_ref[blocks - 1 - b, pl.ds(first - b * rows, last - first), :]
             first = last
         send(joined.at[pl.ds(j * step, step)], out_hbm.at[pl.ds(j * step, step)])
     for i in range(small):
@@ -154,7 +170,7 @@
     got = exchange(sent, "plane")
     part = jnp.sum(got.astype(jnp.float32), axis=0)
     sent = part.reshape(Z, shard_rows, width).astype(jnp.float16)
-    got = exchange(sent[::-1], "z", turned=True)
+    got = exchange_z(listed_z(sent))
     gradient = jnp.sum(got.astype(jnp.float32), axis=0)
     first_moment = beta_one * adam_m[0] + (1.0 - beta_one) * gradient
     second_moment = beta_two * adam_v[0] + (1.0 - beta_two) * gradient * gradient
@@ -168,10 +184,10 @@
     new_mom = momentum * outer_mom + delta
     new_global = global_params - outer_rate * (delta + momentum * new_mom)
     mixed = mixing * inner + (1.0 - mixing) * new_global
-    column = exchange(copies_of(mixed.astype(jnp.bfloat16), Z), "z", turned=True)[::-1]
+    column = unlisted_z(exchange_z(copies_of(mixed.astype(jnp.bfloat16), Z)))
     column = column.reshape(Z * shard_rows, width)
     forward_weight, tall, flat = finish(
-        exchange(copies_of(column, PLANE), "plane"),
+        exchange(copies_of(column, PLANE), "plane", turned=True),
         features,
         (mixed, first_moment, second_moment),
         (new_global, new_mom),

time: 97.1 us -> 96.8 us (level)
  the two profiles are of different devices: /device:TPU:16 before, /device:TPU:64 now
where the time goes in v5:
time: 96.8 us; the launch traced here: 96.4 us
  blocking collectives  91.3 us (94%)
  Pallas kernels  3.43 us (4%)
    all_to_all x3, blocking collectives, exchange(): return lax.all_to_all(blocks, axis, 0, 0, axis_index_groups=groups)  52.4 us
    all_to_all x2, blocking collectives, exchange_z(): return lax.all_to_all(listed, 'z', 0, 0, axis_index_groups=groups)  38.9 us
    pallas_call x1, Pallas kernels, product(): pl.pallas_call(product_kernel, out_shape=jax.ShapeDtypeStruct((blocks, ro...  2.33 us

profile of v5, /device:TPU:64, one launch (start us, length us, event | category | flops | bytes accessed | tf_op | source)
XLA Modules:
  0.0 96.4 jit_solution(14617053067457701679)
XLA Ops:
  0.6 2.3 %product.1 = f32[8,516,128]{2,1,0:T(8,128)S(1)} custom-call(bf16[256,4096]{1,0:T(8,128)(2,1)} %bitcast.34, bf16[256,128]{1,0:T(8,128)(2,1)} %bitcast.39), custom_call_target="tpu_custom_call" | custom-call | tf_op jit(solution)/shard_map/product/pallas_call | solution.py:92
  3.0 0.1 convert_element_type.18
  3.1 21.2 %all_to_all.25 = f16[8,516,128]{2,1,0:T(8,128)(2,1)S(1)} all-to-all(f16[8,516,128]{2,1,0:T(8,128)(2,1)S(1)} %convert_element_type.18), channel_id=1, replica_groups=mesh['plane'=8,'z'=12,'island'=8] {'plane'}, dimensions={0} | all-to-all | bytes 2113536 | tf_op jit(solution)/shard_map/all_to_all | solution.py:31
  24.3 0.1 convert_reduce_fusion
  24.5 0.0 copy-start
  24.5 0.0 copy-start.1
  24.5 0.0 copy-start.3
  24.5 0.0 copy-start.4
  24.6 0.1 convert_element_type.21
  24.6 0.0 copy-start.2
  24.7 23.1 %all_to_all.26 = f16[12,43,128]{2,1,0:T(8,128)(2,1)S(1)} all-to-all(f16[12,43,128]{2,1,0:T(8,128)(2,1)S(1)} %bitcast.36), channel_id=1, replica_groups={{88,40,80,32,72,24,64,16,56,8,48,0},{89,41,81,33,73,25,65,17,57,9,49,1}..., dimensions={0} | all-to-all | bytes 264192 | tf_op jit(solution)/shard_map/all_to_all | solution.py:37
  47.8 0.0 copy-done
  47.8 0.0 copy-done.1
  47.8 0.0 copy-done.3
  47.9 0.0 copy-done.4
  47.9 13.2 %all_to_all.27 = f32[8,43,128]{2,1,0:T(8,128)S(1)} all-to-all(f32[8,43,128]{2,1,0:T(8,128)S(1)} %broadcast_in_dim.10), channel_id=1, replica_groups={{7,6,5,4,3,2,1,0},{15,14,13,12,11,10,9,8},{23,22,21,20,19,18,17,16},{31..., dimensions={0} | all-to-all | bytes 352256 | tf_op jit(solution)/shard_map/all_to_all | solution.py:31
  61.1 0.0 copy-done.2
  61.2 15.8 %all_to_all.28 = bf16[12,43,128]{2,1,0:T(8,128)(2,1)S(1)} all-to-all(bf16[12,43,128]{2,1,0:T(8,128)(2,1)S(1)} %broadcast_in_dim.11), channel_id=1, replica_groups={{88,40,80,32,72,24,64,16,56,8,48,0},{89,41,81,33,73,25,65,17,57,9,49,1}..., dimensions={0} | all-to-all | bytes 264192 | tf_op jit(solution)/shard_map/all_to_all | solution.py:37
  77.1 0.1 broadcast_in_dim.24
  77.2 0.1 broadcast_in_dim.25
  77.3 18.0 %all_to_all.29.refs_0_ = bf16[8,516,128]{2,1,0:T(8,128)(2,1)S(1)} all-to-all(bf16[8,516,128]{2,1,0:T(8,128)(2,1)S(1)} %broadcast_in_dim.25), channel_id=1, replica_groups={{672,576,480,384,288,192,96,0},{673,577,481,385,289,193,97,1},{674,578,..., dimensions={0} | all-to-all | bytes 2113536 | tf_op jit(solution)/shard_map/all_to_all | solution.py:31
  95.3 1.1 %finish.1 = (bf16[4096,128]{1,0:T(8,128)(2,1)}, f32[43,1,128]{2,1,0:T(1,128)}, f32[43,1,128]{2,1,0:T(1,128)}, f32[43,1,128]{2,1,0:T(1,128)}, f32[43,128]{1,0:T(8,128)}, /*index=5*/f32[43,128]{1,0:T(8,128)}) custom-call(bf16[8,516,128]{2,1,0:T(8,128)(2,1)S(1)} %all_to_all.29.refs_0_, f32[43,128]{1,0:T(8,128)S(1)} %get-tuple-element.19.refs_1_, ...), custom_call_target="tpu_custom_call" | custom-call | tf_op jit(solution)/shard_map/finish/pallas_call | solution.py:144
  (11 shorter events, 0.3 us)
Async XLA Ops:
  24.5 23.3 %copy-start = (f32[43,128]{1,0:T(8,128)S(1)}, f32[43,128]{1,0:T(8,128)}, u32[]{:S(2)}) copy-start(f32[43,128]{1,0:T(8,128)} %param.12) | copy-start | bytes 66052
  24.5 23.3 %copy-start.1 = (f32[1,43,128]{2,0,1:T(1,128)S(1)}, f32[1,43,128]{2,0,1:T(1,128)}, u32[]{:S(2)}) copy-start(f32[1,43,128]{2,0,1:T(1,128)} %param.9) | copy-start | bytes 66052
  24.5 23.3 %copy-start.3 = (f32[1,43,128]{2,0,1:T(1,128)S(1)}, f32[1,43,128]{2,0,1:T(1,128)}, u32[]{:S(2)}) copy-start(f32[1,43,128]{2,0,1:T(1,128)} %param.10) | copy-start | bytes 66052
  24.5 23.3 %copy-start.4 = (f32[1,43,128]{2,0,1:T(1,128)S(1)}, f32[1,43,128]{2,0,1:T(1,128)}, u32[]{:S(2)}) copy-start(f32[1,43,128]{2,0,1:T(1,128)} %param.11) | copy-start | bytes 66052
  24.6 36.5 %copy-start.2 = (f32[43,128]{1,0:T(8,128)S(1)}, f32[43,128]{1,0:T(8,128)}, u32[]{:S(2)}) copy-start(f32[43,128]{1,0:T(8,128)} %param.13) | copy-start | bytes 66052

commit v6 on v5

--- a/solution.py
+++ b/solution.py
@@ -118,6 +118,12 @@
         copies.append(pltpu.make_async_copy(source, target, left.at[len(copies)]))
         copies[-1].start()
 
+    for i in range(small):
+        if i < tall:
+            upright[i, :, 0, :] = arrays[i][...]
+            send(upright.at[i], outs[i])
+        else:
+            send(arrays[i], outs[i])
     for j in range(blocks):
         first = j * step
         while first < (j + 1) * step:
@@ -126,12 +132,6 @@
             joined[pl.ds(first, last - first), :] = blocks_ref[blocks - 1 - b, pl.ds(first - b * rows, last - first), :]
             first = last
         send(joined.at[pl.ds(j * step, step)], out_hbm.at[pl.ds(j * step, step)])
-    for i in range(small):
-        if i < tall:
-            upright[i, :, 0, :] = arrays[i][...]
-            send(upright.at[i], outs[i])
-        else:
-            send(arrays[i], outs[i])
     for copy in copies:
         copy.wait()
 

time: 96.8 us -> 96.8 us (level)
  no operation moved by 1% of the time
where the time goes in v6:
time: 96.8 us; the launch traced here: 96.5 us
  blocking collectives  91.3 us (94%)
  Pallas kernels  3.47 us (4%)
    all_to_all x3, blocking collectives, exchange(): return lax.all_to_all(blocks, axis, 0, 0, axis_index_groups=groups)  52.4 us
    all_to_all x2, blocking collectives, exchange_z(): return lax.all_to_all(listed, 'z', 0, 0, axis_index_groups=groups)  38.9 us
    pallas_call x1, Pallas kernels, product(): pl.pallas_call(product_kernel, out_shape=jax.ShapeDtypeStruct((blocks, ro...  2.33 us

profile of v6, /device:TPU:64, one launch (start us, length us, event | category | flops | bytes accessed | tf_op | source)
XLA Modules:
  0.0 96.5 jit_solution(14461658249761269694)
XLA Ops:
  0.6 2.3 %product.1 = f32[8,516,128]{2,1,0:T(8,128)S(1)} custom-call(bf16[256,4096]{1,0:T(8,128)(2,1)} %bitcast.34, bf16[256,128]{1,0:T(8,128)(2,1)} %bitcast.39), custom_call_target="tpu_custom_call" | custom-call | tf_op jit(solution)/shard_map/product/pallas_call | solution.py:92
  3.0 0.1 convert_element_type.18
  3.1 21.2 %all_to_all.25 = f16[8,516,128]{2,1,0:T(8,128)(2,1)S(1)} all-to-all(f16[8,516,128]{2,1,0:T(8,128)(2,1)S(1)} %convert_element_type.18), channel_id=1, replica_groups=mesh['plane'=8,'z'=12,'island'=8] {'plane'}, dimensions={0} | all-to-all | bytes 2113536 | tf_op jit(solution)/shard_map/all_to_all | solution.py:31
  24.3 0.1 convert_reduce_fusion
  24.5 0.0 copy-start
  24.5 0.0 copy-start.1
  24.5 0.0 copy-start.3
  24.5 0.0 copy-start.4
  24.6 0.1 convert_element_type.21
  24.6 0.0 copy-start.2
  24.7 23.1 %all_to_all.26 = f16[12,43,128]{2,1,0:T(8,128)(2,1)S(1)} all-to-all(f16[12,43,128]{2,1,0:T(8,128)(2,1)S(1)} %bitcast.36), channel_id=1, replica_groups={{88,40,80,32,72,24,64,16,56,8,48,0},{89,41,81,33,73,25,65,17,57,9,49,1}..., dimensions={0} | all-to-all | bytes 264192 | tf_op jit(solution)/shard_map/all_to_all | solution.py:37
  47.8 0.0 copy-done
  47.8 0.0 copy-done.1
  47.8 0.0 copy-done.3
  47.9 0.0 copy-done.4
  47.9 13.2 %all_to_all.27 = f32[8,43,128]{2,1,0:T(8,128)S(1)} all-to-all(f32[8,43,128]{2,1,0:T(8,128)S(1)} %broadcast_in_dim.10), channel_id=1, replica_groups={{7,6,5,4,3,2,1,0},{15,14,13,12,11,10,9,8},{23,22,21,20,19,18,17,16},{31..., dimensions={0} | all-to-all | bytes 352256 | tf_op jit(solution)/shard_map/all_to_all | solution.py:31
  61.1 0.0 copy-done.2
  61.2 15.8 %all_to_all.28 = bf16[12,43,128]{2,1,0:T(8,128)(2,1)S(1)} all-to-all(bf16[12,43,128]{2,1,0:T(8,128)(2,1)S(1)} %broadcast_in_dim.11), channel_id=1, replica_groups={{88,40,80,32,72,24,64,16,56,8,48,0},{89,41,81,33,73,25,65,17,57,9,49,1}..., dimensions={0} | all-to-all | bytes 264192 | tf_op jit(solution)/shard_map/all_to_all | solution.py:37
  77.1 0.1 broadcast_in_dim.24
  77.2 0.1 broadcast_in_dim.25
  77.3 18.0 %all_to_all.29.refs_0_ = bf16[8,516,128]{2,1,0:T(8,128)(2,1)S(1)} all-to-all(bf16[8,516,128]{2,1,0:T(8,128)(2,1)S(1)} %broadcast_in_dim.25), channel_id=1, replica_groups={{672,576,480,384,288,192,96,0},{673,577,481,385,289,193,97,1},{674,578,..., dimensions={0} | all-to-all | bytes 2113536 | tf_op jit(solution)/shard_map/all_to_all | solution.py:31
  95.3 1.1 %finish.1 = (bf16[4096,128]{1,0:T(8,128)(2,1)}, f32[43,1,128]{2,1,0:T(1,128)}, f32[43,1,128]{2,1,0:T(1,128)}, f32[43,1,128]{2,1,0:T(1,128)}, f32[43,128]{1,0:T(8,128)}, /*index=5*/f32[43,128]{1,0:T(8,128)}) custom-call(bf16[8,516,128]{2,1,0:T(8,128)(2,1)S(1)} %all_to_all.29.refs_0_, f32[43,128]{1,0:T(8,128)S(1)} %get-tuple-element.19.refs_1_, ...), custom_call_target="tpu_custom_call" | custom-call | tf_op jit(solution)/shard_map/finish/pallas_call | solution.py:144
  (11 shorter events, 0.3 us)
Async XLA Ops:
  24.5 23.3 %copy-start = (f32[43,128]{1,0:T(8,128)S(1)}, f32[43,128]{1,0:T(8,128)}, u32[]{:S(2)}) copy-start(f32[43,128]{1,0:T(8,128)} %param.12) | copy-start | bytes 66052
  24.5 23.3 %copy-start.1 = (f32[1,43,128]{2,0,1:T(1,128)S(1)}, f32[1,43,128]{2,0,1:T(1,128)}, u32[]{:S(2)}) copy-start(f32[1,43,128]{2,0,1:T(1,128)} %param.9) | copy-start | bytes 66052
  24.5 23.3 %copy-start.3 = (f32[1,43,128]{2,0,1:T(1,128)S(1)}, f32[1,43,128]{2,0,1:T(1,128)}, u32[]{:S(2)}) copy-start(f32[1,43,128]{2,0,1:T(1,128)} %param.10) | copy-start | bytes 66052
  24.5 23.3 %copy-start.4 = (f32[1,43,128]{2,0,1:T(1,128)S(1)}, f32[1,43,128]{2,0,1:T(1,128)}, u32[]{:S(2)}) copy-start(f32[1,43,128]{2,0,1:T(1,128)} %param.11) | copy-start | bytes 66052
  24.6 36.5 %copy-start.2 = (f32[43,128]{1,0:T(8,128)S(1)}, f32[43,128]{1,0:T(8,128)}, u32[]{:S(2)}) copy-start(f32[43,128]{1,0:T(8,128)} %param.13) | copy-start | bytes 66052
